TPU v7x, 32 devices: a whole 2x2x4 slice. The times are simulated.
32 devices in a mesh: tm: 4 (over z), space: 2 (over y), clip: 4 (over x, core).
Axes of the slice: x: 2, y: 2, z: 4, core: 2. Of those that a mesh axis runs over, the one named last changes fastest.
Arguments:
- activations: bfloat16 [96, 64, 1408], P(('clip', 'tm'), 'space'), parts along dimension 0, may hold values from -200 to 200
- attn_gain: float32 [1408], replicated, may hold values from 0.5 to 2
- attn_shift: float32 [1408], replicated, may hold values from -3 to 3
- w_qkv: bfloat16 [1408, 4224], replicated, may hold values from -4 to 4
- b_qkv: float32 [4224], replicated, may hold values from -3 to 3
- w_out: bfloat16 [1408, 1408], replicated, may hold values from -2.5 to 2.5
- b_out: float32 [1408], replicated, may hold values from -3 to 3
- final_gain: float32 [1408], replicated, may hold values from 0.5 to 2
- final_shift: float32 [1408], replicated, may hold values from -3 to 3
- mask_tokens: int32 [32, 192], P('clip'), parts along dimension 0, may hold values from -1 to 1535, as said below
- assignment: int32 [32], P('clip'), parts along dimension 0, may hold values from 0 to 7, each once
Outputs:
- targets: bfloat16 [32, 192, 1408], P(('clip', 'tm', 'space')), parts along dimension 0
There are 4 independent parts, one for each index of `clip`. A program takes and returns all parts, laid end to end along the dimension named above; an argument that names none is the same for every part. Nothing has to cross between parts.
Inputs may be any that keep to these rules, and one draw needn't show every extreme that they name: `mask_tokens`: each row lists distinct tokens, no token in two rows; its listed entries come first in no fixed order, then -1 to the end. The block of tokens of one device (temporal positions k * 6 to k * 6 + 5 and patch positions m * 32 to m * 32 + 31) gives at most 24 entries to one row; in some row every such block gives exactly 24, so that row is full. `assignment`: each owner once.
All inputs are finite; a program needn't handle non-finite values.
Results may differ from a plain program's by a relative error of at most 0.0085.
The roundings to bfloat16 on the way count: a program that leaves them out, or rounds other values in their place, can miss the bound.
Values may be sent and summed in bfloat16 or wider, within the bound.
A program may use at most 128 MiB of HBM per device.

v0:
```python
import functools
import math

import jax
import jax.numpy as jnp
import numpy as np
from jax import lax
from jax.experimental import pallas as pl
from jax.experimental.pallas import tpu as pltpu
from jax.sharding import PartitionSpec as P

HEADS = 16


EPSILON = 1e-06
FLOOR_SCORE = -1e30


def layer_norm(values, ln_gain, ln_shift):
    centre = jnp.mean(values, axis=-1, keepdims=True)
    deviation = values - centre
    variance = jnp.mean(deviation * deviation, axis=-1, keepdims=True)
    return deviation * lax.rsqrt(variance + EPSILON) * ln_gain + ln_shift


def start_state(query_heads):
    query_count, head_count, head_width = query_heads.shape
    return (
        jnp.full((head_count, query_count), FLOOR_SCORE, jnp.float32),
        jnp.zeros((head_count, query_count), jnp.float32),
        jnp.zeros((head_count, query_count, head_width), jnp.float32),
    )


def finish_state(carried_state):
    running_max, running_total, running_sum = carried_state
    return jnp.transpose(running_sum / running_total[:, :, None], (1, 0, 2)).astype(jnp.bfloat16)


def make_attend(query_heads):
    query_count, head_count, head_width = query_heads.shape
    score_scale = 1.0 / math.sqrt(head_width)

    def one_block(carried_state, kv_block):
        running_max, running_total, running_sum = carried_state
        block_length = kv_block.shape[1]
        key_rows = kv_block[0].reshape(block_length, head_count, head_width)
        value_rows = kv_block[1].reshape(block_length, head_count, head_width)
        scores = (
            jnp.einsum("qhe,khe->hqk", query_heads, key_rows, preferred_element_type=jnp.float32)
            * score_scale
        )
        new_max = jnp.maximum(running_max, jnp.max(scores, axis=-1))
        factor = jnp.exp(running_max - new_max)
        weights = jnp.exp(scores - new_max[:, :, None])
        running_total = running_total * factor + jnp.sum(weights, axis=-1)
        running_sum = running_sum * factor[:, :, None] + jnp.einsum(
            "hqk,khe->hqe",
            weights.astype(jnp.bfloat16),
            value_rows,
            preferred_element_type=jnp.float32,
        )
        return (new_max, running_total, running_sum)

    def attend(carried_state, key_piece, first_row):
        length = key_piece.shape[1]
        block_rows = length
        while block_rows > 1024 and block_rows % 2 == 0:
            block_rows = block_rows // 2

        def advance(position, carried):
            kv_block = lax.dynamic_slice_in_dim(key_piece, position * block_rows, block_rows, 1)
            return one_block(carried, kv_block)

        return lax.fori_loop(0, length // block_rows, advance, carried_state)

    return attend


def local(
    activations,
    attn_gain,
    attn_shift,
    w_qkv,
    b_qkv,
    w_out,
    b_out,
    final_gain,
    final_shift,
    mask_tokens,
    assignment,
):
    frame_count, patch_count, model_width = activations.shape
    local_rows = frame_count * patch_count
    head_width = model_width // HEADS
    tokens_flat = activations.reshape(local_rows, model_width)
    normed_in = layer_norm(tokens_flat.astype(jnp.float32), attn_gain, attn_shift).astype(
        jnp.bfloat16
    )
    projected = (jnp.dot(normed_in, w_qkv, preferred_element_type=jnp.float32) + b_qkv).astype(
        jnp.bfloat16
    )
    query_rows = projected[:, :model_width]
    paired = jnp.stack(
        (projected[:, model_width : 2 * model_width], projected[:, 2 * model_width :])
    )
    groups = lax.axis_size("space")
    group_heads = HEADS // groups
    stacked = jnp.stack((query_rows, paired[0], paired[1])).reshape(
        3, local_rows, groups, group_heads, head_width
    )
    swapped = lax.all_to_all(stacked, "space", split_axis=2, concat_axis=1, tiled=True)
    gathered_rows = swapped.shape[1]
    kept_heads = swapped.shape[3]
    query_heads = swapped[0].reshape(gathered_rows, kept_heads, head_width)
    kv_rows = swapped[1:].reshape(2, gathered_rows, kept_heads * head_width)
    time_state = make_attend(query_heads)(
        start_state(query_heads), lax.all_gather(kv_rows, "tm", axis=1, tiled=True), jnp.int32(0)
    )
    head_output = finish_state(time_state).reshape(gathered_rows, 1, kept_heads, head_width)
    merged = lax.all_to_all(head_output, "space", split_axis=0, concat_axis=1, tiled=True)
    attended = merged.reshape(local_rows, model_width)
    hidden = (
        tokens_flat.astype(jnp.float32)
        + jnp.dot(attended, w_out, preferred_element_type=jnp.float32)
        + b_out
    ).astype(jnp.bfloat16)
    normed = layer_norm(hidden.astype(jnp.float32), final_gain, final_shift).astype(jnp.bfloat16)
    owners = mask_tokens.shape[0]
    capacity = mask_tokens.shape[1]
    per_source = capacity // owners
    spaces = lax.axis_size("space")
    spatial = patch_count * spaces
    own_index = lax.axis_index("tm") * spaces + lax.axis_index("space")
    owner_lists = jnp.take(mask_tokens, assignment, axis=0)
    listed = owner_lists >= 0
    clipped = jnp.maximum(owner_lists, 0)
    token_frame = clipped // spatial
    token_patch = clipped % spatial
    home_device = token_frame // frame_count * spaces + token_patch // patch_count
    local_row = token_frame % frame_count * patch_count + token_patch % patch_count
    mine = listed & (home_device == own_index)
    slot_index = jnp.cumsum(mine.astype(jnp.int32), axis=1) - 1
    wanted = mine[:, None, :] & (
        slot_index[:, None, :] == jnp.arange(per_source, dtype=jnp.int32)[None, :, None]
    )
    picks = jnp.sum(jnp.where(wanted, local_row[:, None, :], 0), axis=-1)
    present = jnp.any(wanted, axis=-1)
    own_home = lax.dynamic_index_in_dim(home_device, own_index, 0, keepdims=False)
    own_listed = lax.dynamic_index_in_dim(listed, own_index, 0, keepdims=False)
    entry_order = jnp.arange(capacity, dtype=jnp.int32)
    earlier = (
        (entry_order[:, None] < entry_order[None, :])
        & own_listed[:, None]
        & (own_home[:, None] == own_home[None, :])
    )
    entry_rank = jnp.sum(earlier.astype(jnp.int32), axis=0)
    where_from = jnp.where(own_listed, own_home * per_source + entry_rank, 0)
    outgoing = jnp.where(
        present[:, :, None], jnp.take(normed, picks, axis=0), jnp.zeros((), jnp.bfloat16)
    )
    arrived = lax.all_to_all(outgoing, ("tm", "space"), split_axis=0, concat_axis=0, tiled=True)
    row_table = arrived.reshape(owners * per_source, model_width)
    placed = jnp.take(row_table, where_from, axis=0)
    return jnp.where(own_listed[:, None], placed, jnp.zeros((), jnp.bfloat16))[None]


LANES = 128
WINDOW = 256
VMEM_LIMIT = 60 * 1024 * 1024
MESH = pl.DeviceIdType.MESH


def norm_rows(values, gain, shift):
    return layer_norm(values.astype(jnp.float32), gain, shift).astype(jnp.bfloat16)


def fused_kernel(
    times,
    head_width,
    x_ref,
    gain_flat,
    shift_flat,
    w_qkv_ref,
    b_qkv_flat,
    w_out_ref,
    b_out_flat,
    final_gain_flat,
    final_shift_flat,
    lists_ref,
    assignment_ref,
    columns_ref,
    out_ref,
    x_all,
    kv_all,
    w_qkv,
    w_out,
    normed,
    queries,
    attended,
    b_qkv_ref,
    vectors,
    local_sem,
    up_send,
    down_send,
    side_send,
    line_recv,
    side_recv,
    mate_sem,
):
    me = lax.axis_index("tm")
    side = lax.axis_index("space")
    other = 1 - side
    rows, width = x_ref.shape
    half_rows = rows // 2
    mate = me + 1 - 2 * lax.rem(me, 2)
    load_x = [
        pltpu.make_async_copy(
            x_ref.at[pl.ds(half * half_rows, half_rows)],
            x_all.at[me, side, half],
            local_sem.at[2 + half],
        )
        for half in range(2)
    ]
    load_qkv = pltpu.make_async_copy(w_qkv_ref, w_qkv, local_sem.at[0])
    load_out = pltpu.make_async_copy(w_out_ref, w_out, local_sem.at[1])
    for load in load_x:
        load.start()
    load_qkv.start()
    load_out.start()

    has_up = me < times - 1
    has_down = me > 0

    barrier = pltpu.get_barrier_semaphore()
    pl.semaphore_signal(barrier, inc=1, device_id={"space": other}, device_id_type=MESH)

    @pl.when(has_up)
    def _():
        pl.semaphore_signal(barrier, inc=1, device_id={"tm": me + 1}, device_id_type=MESH)

    @pl.when(has_down)
    def _():
        pl.semaphore_signal(barrier, inc=1, device_id={"tm": me - 1}, device_id_type=MESH)

    pl.semaphore_wait(barrier, 1 + has_up.astype(jnp.int32) + has_down.astype(jnp.int32))

    def up_copy(source, block, half):
        return pltpu.make_async_remote_copy(
            source, x_all.at[block, side, half], up_send.at[block, half],
            line_recv.at[block, half], device_id={"tm": me + 1}, device_id_type=MESH,
        )

    def down_copy(source, block, half):
        return pltpu.make_async_remote_copy(
            source, x_all.at[block, side, half], down_send.at[block, half],
            line_recv.at[block, half], device_id={"tm": me - 1}, device_id_type=MESH,
        )

    def side_copy(block, half, from_side, source=None):
        place = x_all.at[block, from_side, half]
        return pltpu.make_async_remote_copy(
            place if source is None else source, place, side_send.at[block, half],
            side_recv.at[block, half], device_id={"space": other}, device_id_type=MESH,
        )

    def mate_copy(block):
        place = x_all.at[block, other, 1]
        return pltpu.make_async_remote_copy(
            place, place, mate_sem.at[0], mate_sem.at[1],
            device_id={"tm": mate}, device_id_type=MESH,
        )

    for half in range(2):
        own_half = x_ref.at[pl.ds(half * half_rows, half_rows)]

        @pl.when(has_up)
        def _():
            up_copy(own_half, me, half).start()

        @pl.when(has_down)
        def _():
            down_copy(own_half, me, half).start()

        side_copy(me, half, side, own_half).start()

    b_qkv_ref[...] = b_qkv_flat[...].reshape(1, 3 * width)
    flats = (gain_flat, shift_flat, b_out_flat, final_gain_flat, final_shift_flat)
    for place, flat in enumerate(flats):
        vectors[place : place + 1, :] = flat[...].reshape(1, width)
    gain_ref, shift_ref, b_out_ref, final_gain_ref, final_shift_ref = (
        vectors.at[place : place + 1, :] for place in range(len(flats))
    )

    def send_aside(block, half):
        if half == 0:
            side_copy(block, half, side).start()
        else:

            @pl.when(block != mate)
            def _():
                side_copy(block, half, side).start()

    def arrive_and_forward(step, half):
        below, above = me - step, me + step

        @pl.when(below >= 0)
        def _():
            held = x_all.at[below, side, half]
            up_copy(held, below, half).wait_recv()

            @pl.when(has_up)
            def _():
                up_copy(held, below, half).start()

            send_aside(below, half)

        @pl.when(above < times)
        def _():
            held = x_all.at[above, side, half]
            down_copy(held, above, half).wait_recv()

            @pl.when(has_down)
            def _():
                down_copy(held, above, half).start()

            send_aside(above, half)

    reach = jnp.minimum(me, times - 1 - me)
    toward = mate - me

    def ordered(place):
        if place == 0:
            return me
        near = me + ((place + 1) // 2) * (toward if place % 2 else -toward)
        far_step = place - reach
        far = jnp.where(2 * me > times - 1, me - far_step, me + far_step)
        return jnp.where(place <= 2 * reach, near, far)

    tiles = 2 * width // WINDOW

    def project(pieces):
        count = len(pieces)
        for place, (block, from_side, half) in enumerate(pieces):
            normed[place * half_rows : (place + 1) * half_rows, :] = norm_rows(
                x_all[block, from_side, half], gain_ref[...], shift_ref[...]
            )

        def one_tile(tile, carried):
            start = pl.multiple_of(tile * WINDOW, WINDOW)
            shifted = pl.multiple_of(width + tile * WINDOW, LANES)
            made = jnp.dot(
                normed[: count * half_rows, :],
                w_qkv[:, pl.ds(shifted, WINDOW)],
                preferred_element_type=jnp.float32,
            )
            made = (made + b_qkv_ref[:, pl.ds(shifted, WINDOW)]).astype(jnp.bfloat16)
            for place, (block, from_side, half) in enumerate(pieces):
                kv_all[block * 2 + from_side, half, :, pl.ds(start, WINDOW)] = made[
                    place * half_rows : (place + 1) * half_rows, :
                ]
            return carried

        lax.fori_loop(0, tiles, one_tile, 0)

    def from_aside(place):
        block = ordered(place)
        pieces = []
        for half in range(1 if place == 1 else 2):
            side_copy(block, half, other).wait_recv()
            pieces.append((block, other, half))
        return pieces

    for load in load_x:
        load.wait()
    load_qkv.wait()
    project([(me, side, 0), (me, side, 1)])
    last = ordered(times - 1)
    for step in range(1, times - 1):
        arrive_and_forward(step, 0)
        arrive_and_forward(step, 1)
        ready = from_aside(step - 1)
        if step == times - 2:
            mate_copy(me).start()
        project([(ordered(step), side, 0), (ordered(step), side, 1)] + ready)
    arrive_and_forward(times - 1, 0)
    project([(last, side, 0)] + from_aside(times - 2))
    arrive_and_forward(times - 1, 1)
    side_copy(last, 0, other).wait_recv()
    project([(last, side, 1), (last, other, 0)])
    owner = assignment_ref[me * 2 + side]
    list_places = lax.broadcasted_iota(jnp.int32, lists_ref.shape, 0)
    lists = lists_ref[...].astype(jnp.float32)
    token_row = jnp.sum(jnp.where(list_places == owner, lists, 0.0), axis=0, keepdims=True)
    capacity = lists_ref.shape[1]
    diagonal = lax.broadcasted_iota(jnp.int32, (capacity, capacity), 0) == lax.broadcasted_iota(
        jnp.int32, (capacity, capacity), 1
    )
    tokens = jnp.sum(jnp.where(diagonal, token_row, 0.0), axis=1, keepdims=True)

    def pick(block, from_side):
        listed = tokens == columns_ref[pl.ds(block * 2 + from_side, 1), :]
        return jnp.dot(
            listed.astype(jnp.float32).astype(jnp.bfloat16),
            x_all[block, from_side].reshape(rows, width),
            preferred_element_type=jnp.float32,
        )

    picked = pick(0, side)
    for block in range(1, times):
        picked += pick(block, side)

    side_copy(last, 1, other).wait_recv()
    mate_copy(mate).wait_recv()
    project([(last, other, 1), (mate, other, 1)])

    for block in range(times):
        picked += pick(block, other)
    out_ref[0] = picked.astype(jnp.bfloat16)
    queries[...] = (
        jnp.dot(
            norm_rows(picked, gain_ref[...], shift_ref[...]),
            w_qkv[:, :width],
            preferred_element_type=jnp.float32,
        )
        + b_qkv_ref[:, :width]
    ).astype(jnp.bfloat16)
    attended[...] = jnp.zeros_like(attended)
    score_scale = math.log2(math.e) / math.sqrt(head_width)
    all_rows = times * 2 * rows

    def window_of(first):
        return min(first // LANES, width // LANES - 2) * LANES

    groups = []
    head = 0
    while head < HEADS:
        base = window_of(head * head_width)
        count = 1
        while head + count < HEADS and (head + count + 1) * head_width <= base + WINDOW:
            count += 1
        groups.append((base, range(head, head + count)))
        head += count

    for base, heads in groups:
        lane = lax.broadcasted_iota(jnp.int32, (capacity, WINDOW), 1) + base
        inside = [(lane >= h * head_width) & (lane < (h + 1) * head_width) for h in heads]
        window_queries = queries[:, base : base + WINDOW].astype(jnp.float32)
        query = jnp.concatenate(
            [jnp.where(mask, window_queries, 0.0).astype(jnp.bfloat16) for mask in inside]
        )
        keys = kv_all[:, :, :, base : base + WINDOW].reshape(all_rows, WINDOW)
        values = kv_all[:, :, :, width + base : width + base + WINDOW].reshape(all_rows, WINDOW)
        scores = (
            lax.dot_general(
                query, keys, (((1,), (1,)), ((), ())), preferred_element_type=jnp.float32
            )
            * score_scale
        )
        weights = jnp.exp2(scores - jnp.max(scores, axis=1, keepdims=True))
        totals = jnp.sum(weights, axis=1, keepdims=True)
        summed = jnp.dot(weights.astype(jnp.bfloat16), values, preferred_element_type=jnp.float32)
        summed = summed / totals
        for place, mask in enumerate(inside):
            attended[:, base : base + WINDOW] += jnp.where(
                mask, summed[place * capacity : (place + 1) * capacity], 0.0
            )

    load_out.wait()
    hidden = (
        out_ref[0].astype(jnp.float32)
        + jnp.dot(
            attended[...].astype(jnp.bfloat16), w_out[...], preferred_element_type=jnp.float32
        )
        + b_out_ref[...]
    ).astype(jnp.bfloat16)
    final = layer_norm(hidden.astype(jnp.float32), final_gain_ref[...], final_shift_ref[...])
    out_ref[0] = jnp.where(tokens >= 0, final, 0.0).astype(jnp.bfloat16)

    for block in range(times):
        for half in range(2):

            @pl.when(has_up & (block <= me))
            def _():
                up_copy(x_all.at[block, side, half], block, half).wait_send()

            @pl.when(has_down & (block >= me))
            def _():
                down_copy(x_all.at[block, side, half], block, half).wait_send()

            @pl.when((block != mate) | (half == 0))
            def _():
                side_copy(block, half, side).wait_send()

    mate_copy(me).wait_send()


def fits_fused(times, spaces, rows, width, capacity):
    all_rows = times * spaces * rows
    held = 2 * (all_rows * width * 3 + width * width * 4 + 2 * rows * width)
    held += 4 * capacity * (width * 2 + all_rows * 3)
    return (
        spaces == 2
        and held < VMEM_LIMIT
        and width % LANES == 0
        and width // HEADS <= LANES
        and rows % 32 == 0
        and times % 2 == 0
        and times > 2
    )


def fused_local(
    activations,
    attn_gain,
    attn_shift,
    w_qkv,
    b_qkv,
    w_out,
    b_out,
    final_gain,
    final_shift,
    mask_tokens,
    assignment,
):
    frames, patches, width = activations.shape
    rows = frames * patches
    times = lax.axis_size("tm")
    spaces = lax.axis_size("space")
    if not fits_fused(times, spaces, rows, width, mask_tokens.shape[1]):
        return local(
            activations, attn_gain, attn_shift, w_qkv, b_qkv, w_out, b_out,
            final_gain, final_shift, mask_tokens, assignment,
        )
    capacity = mask_tokens.shape[1]
    order = np.arange(times * frames * spaces * patches).reshape(times, frames, spaces, patches)
    columns = order.transpose(0, 2, 1, 3).reshape(times * spaces, -1).astype(np.float32)
    vmem = pl.BlockSpec(memory_space=pltpu.VMEM)
    hbm = pl.BlockSpec(memory_space=pl.ANY)
    smem = pl.BlockSpec(memory_space=pltpu.SMEM)
    return pl.pallas_call(
        functools.partial(fused_kernel, times, width // HEADS),
        out_shape=jax.ShapeDtypeStruct((1, capacity, width), jnp.bfloat16),
        in_specs=[vmem, vmem, vmem, hbm, vmem, hbm, vmem, vmem, vmem, vmem, smem, vmem],
        out_specs=vmem,
        scratch_shapes=[
            pltpu.VMEM((times, spaces, 2, rows // 2, width), jnp.bfloat16),
            pltpu.VMEM((times * spaces, 2, rows // 2, 2 * width), jnp.bfloat16),
            pltpu.VMEM(w_qkv.shape, jnp.bfloat16),
            pltpu.VMEM(w_out.shape, jnp.bfloat16),
            pltpu.VMEM((2 * rows, width), jnp.bfloat16),
            pltpu.VMEM((capacity, width), jnp.bfloat16),
            pltpu.VMEM((capacity, width), jnp.float32),
            pltpu.VMEM((1, 3 * width), jnp.float32),
            pltpu.VMEM((5, width), jnp.float32),
            pltpu.SemaphoreType.DMA((4,)),
            pltpu.SemaphoreType.DMA((times, 2)),
            pltpu.SemaphoreType.DMA((times, 2)),
            pltpu.SemaphoreType.DMA((times, 2)),
            pltpu.SemaphoreType.DMA((times, 2)),
            pltpu.SemaphoreType.DMA((times, 2)),
            pltpu.SemaphoreType.DMA((2,)),
        ],
        compiler_params=pltpu.CompilerParams(
            collective_id=0, has_side_effects=True, vmem_limit_bytes=VMEM_LIMIT
        ),
    )(
        activations.reshape(rows, width),
        attn_gain,
        attn_shift,
        w_qkv,
        b_qkv,
        w_out,
        b_out,
        final_gain,
        final_shift,
        mask_tokens,
        assignment,
        jnp.asarray(columns),
    )


def solution(mesh):
    in_specs = (
        P(("clip", "tm"), "space", None),
        P(),
        P(),
        P(),
        P(),
        P(),
        P(),
        P(),
        P(),
        P("clip", None),
        P("clip"),
    )
    out_specs = P(("clip", "tm", "space"), None, None)
    return jax.shard_map(fused_local, mesh=mesh, in_specs=in_specs, out_specs=out_specs, check_vma=False)
```

profile of v0, /device:TPU:0, one launch (start us, length us, event | category | flops | bytes accessed | tf_op | source)
XLA Modules:
  0.0 67.1 jit_solution(13513077069377411841)
XLA Ops:
  0.0 65.2 %shard_map.118 = bf16[1,192,1408]{2,1,0:T(8,128)(2,1)} custom-call(bf16[192,1408]{1,0:T(8,128)(2,1)} %bitcast.1, f32[1408]{0:T(1024)} %gain_flat.1, f32[1408]{0:T(1024)} %shift_flat.1, bf16[1408,4224]{1,0:T(8,128)(2,1)} %w_qkv_ref.1, f32[4224]{0:T(1024)} %b_qkv_flat.1, bf16[1408,1408]{1,0:T(8,128)(2,1)} %w_out_ref.1, f32[1408]{0:T(1024)} %b_out_flat.1, ...), custom_call_target="tpu_custom_call" | custom-call | tf_op jit(solution)/shard_map/pallas_call | solution.py:541
  65.2 1.9 %copy.14 = bf16[1,192,1408]{2,1,0:T(8,128)(2,1)} copy(bf16[1,192,1408]{2,1,0:T(8,128)(2,1)} %shard_map.118) | data formatting | bytes 1081344
where the time goes:
time: 67.2 us; the launch traced here: 67.1 us
  Pallas kernels  65.2 us (97%)
  local copies, waits for them, and re-layouts  1.89 us (3%)
    pallas_call x1, Pallas kernels, fused_local(): pl.pallas_call(functools.partial(fused_kernel, times, width // HEADS), ou...  65.2 us
    unnamed x1, local copies, waits for them, and re-layouts  1.89 us

commit v1 on v0

--- a/solution.py
+++ b/solution.py
@@ -337,7 +337,7 @@
         far = jnp.where(2 * me > times - 1, me - far_step, me + far_step)
         return jnp.where(place <= 2 * reach, near, far)
 
-    tiles = 2 * width // WINDOW
+    tiles = 2
 
     def project(pieces):
         count = len(pieces)
@@ -347,16 +347,16 @@
             )
 
         def one_tile(tile, carried):
-            start = pl.multiple_of(tile * WINDOW, WINDOW)
-            shifted = pl.multiple_of(width + tile * WINDOW, LANES)
+            start = pl.multiple_of(tile * width, LANES)
+            shifted = pl.multiple_of(width + tile * width, LANES)
             made = jnp.dot(
                 normed[: count * half_rows, :],
-                w_qkv[:, pl.ds(shifted, WINDOW)],
+                w_qkv[:, pl.ds(shifted, width)],
                 preferred_element_type=jnp.float32,
             )
-            made = (made + b_qkv_ref[:, pl.ds(shifted, WINDOW)]).astype(jnp.bfloat16)
+            made = (made + b_qkv_ref[:, pl.ds(shifted, width)]).astype(jnp.bfloat16)
             for place, (block, from_side, half) in enumerate(pieces):
-                kv_all[block * 2 + from_side, half, :, pl.ds(start, WINDOW)] = made[
+                kv_all[block * 2 + from_side, half, :, pl.ds(start, width)] = made[
                     place * half_rows : (place + 1) * half_rows, :
                 ]
             return carried

time: 67.2 us -> 65.6 us (0.976)
  Pallas kernels: 65.2 us -> 63.6 us
    pallas_call x1, Pallas kernels: 65.2 us -> 63.6 us  [fused_local(): pl.pallas_call(functools.partial(fused_kernel, times, width // HEADS), ou...]
where the time goes in v1:
time: 65.6 us; the launch traced here: 65.5 us
  Pallas kernels  63.6 us (97%)
  local copies, waits for them, and re-layouts  1.89 us (3%)
    pallas_call x1, Pallas kernels, fused_local(): pl.pallas_call(functools.partial(fused_kernel, times, width // HEADS), ou...  63.6 us
    unnamed x1, local copies, waits for them, and re-layouts  1.89 us

profile of v1, /device:TPU:0, one launch (start us, length us, event | category | flops | bytes accessed | tf_op | source)
XLA Modules:
  0.0 65.5 jit_solution(5977548916325308405)
XLA Ops:
  0.0 63.6 %shard_map.118 = bf16[1,192,1408]{2,1,0:T(8,128)(2,1)} custom-call(bf16[192,1408]{1,0:T(8,128)(2,1)} %bitcast.1, f32[1408]{0:T(1024)} %gain_flat.1, f32[1408]{0:T(1024)} %shift_flat.1, bf16[1408,4224]{1,0:T(8,128)(2,1)} %w_qkv_ref.1, f32[4224]{0:T(1024)} %b_qkv_flat.1, bf16[1408,1408]{1,0:T(8,128)(2,1)} %w_out_ref.1, f32[1408]{0:T(1024)} %b_out_flat.1, ...), custom_call_target="tpu_custom_call" | custom-call | tf_op jit(solution)/shard_map/pallas_call | solution.py:541
  63.6 1.9 %copy.14 = bf16[1,192,1408]{2,1,0:T(8,128)(2,1)} copy(bf16[1,192,1408]{2,1,0:T(8,128)(2,1)} %shard_map.118) | data formatting | bytes 1081344

commit v2 on v1

v2 whole, which is shorter than its diff:
```python
import functools
import math

import jax
import jax.numpy as jnp
from jax import lax
from jax.experimental import pallas as pl
from jax.experimental.pallas import tpu as pltpu
from jax.sharding import PartitionSpec as P

HEADS = 16


EPSILON = 1e-06
FLOOR_SCORE = -1e30


def layer_norm(values, ln_gain, ln_shift):
    centre = jnp.mean(values, axis=-1, keepdims=True)
    deviation = values - centre
    variance = jnp.mean(deviation * deviation, axis=-1, keepdims=True)
    return deviation * lax.rsqrt(variance + EPSILON) * ln_gain + ln_shift


def start_state(query_heads):
    query_count, head_count, head_width = query_heads.shape
    return (
        jnp.full((head_count, query_count), FLOOR_SCORE, jnp.float32),
        jnp.zeros((head_count, query_count), jnp.float32),
        jnp.zeros((head_count, query_count, head_width), jnp.float32),
    )


def finish_state(carried_state):
    running_max, running_total, running_sum = carried_state
    return jnp.transpose(running_sum / running_total[:, :, None], (1, 0, 2)).astype(jnp.bfloat16)


def make_attend(query_heads):
    query_count, head_count, head_width = query_heads.shape
    score_scale = 1.0 / math.sqrt(head_width)

    def one_block(carried_state, kv_block):
        running_max, running_total, running_sum = carried_state
        block_length = kv_block.shape[1]
        key_rows = kv_block[0].reshape(block_length, head_count, head_width)
        value_rows = kv_block[1].reshape(block_length, head_count, head_width)
        scores = (
            jnp.einsum("qhe,khe->hqk", query_heads, key_rows, preferred_element_type=jnp.float32)
            * score_scale
        )
        new_max = jnp.maximum(running_max, jnp.max(scores, axis=-1))
        factor = jnp.exp(running_max - new_max)
        weights = jnp.exp(scores - new_max[:, :, None])
        running_total = running_total * factor + jnp.sum(weights, axis=-1)
        running_sum = running_sum * factor[:, :, None] + jnp.einsum(
            "hqk,khe->hqe",
            weights.astype(jnp.bfloat16),
            value_rows,
            preferred_element_type=jnp.float32,
        )
        return (new_max, running_total, running_sum)

    def attend(carried_state, key_piece, first_row):
        length = key_piece.shape[1]
        block_rows = length
        while block_rows > 1024 and block_rows % 2 == 0:
            block_rows = block_rows // 2

        def advance(position, carried):
            kv_block = lax.dynamic_slice_in_dim(key_piece, position * block_rows, block_rows, 1)
            return one_block(carried, kv_block)

        return lax.fori_loop(0, length // block_rows, advance, carried_state)

    return attend


def local(
    activations,
    attn_gain,
    attn_shift,
    w_qkv,
    b_qkv,
    w_out,
    b_out,
    final_gain,
    final_shift,
    mask_tokens,
    assignment,
):
    frame_count, patch_count, model_width = activations.shape
    local_rows = frame_count * patch_count
    head_width = model_width // HEADS
    tokens_flat = activations.reshape(local_rows, model_width)
    normed_in = layer_norm(tokens_flat.astype(jnp.float32), attn_gain, attn_shift).astype(
        jnp.bfloat16
    )
    projected = (jnp.dot(normed_in, w_qkv, preferred_element_type=jnp.float32) + b_qkv).astype(
        jnp.bfloat16
    )
    query_rows = projected[:, :model_width]
    paired = jnp.stack(
        (projected[:, model_width : 2 * model_width], projected[:, 2 * model_width :])
    )
    groups = lax.axis_size("space")
    group_heads = HEADS // groups
    stacked = jnp.stack((query_rows, paired[0], paired[1])).reshape(
        3, local_rows, groups, group_heads, head_width
    )
    swapped = lax.all_to_all(stacked, "space", split_axis=2, concat_axis=1, tiled=True)
    gathered_rows = swapped.shape[1]
    kept_heads = swapped.shape[3]
    query_heads = swapped[0].reshape(gathered_rows, kept_heads, head_width)
    kv_rows = swapped[1:].reshape(2, gathered_rows, kept_heads * head_width)
    time_state = make_attend(query_heads)(
        start_state(query_heads), lax.all_gather(kv_rows, "tm", axis=1, tiled=True), jnp.int32(0)
    )
    head_output = finish_state(time_state).reshape(gathered_rows, 1, kept_heads, head_width)
    merged = lax.all_to_all(head_output, "space", split_axis=0, concat_axis=1, tiled=True)
    attended = merged.reshape(local_rows, model_width)
    hidden = (
        tokens_flat.astype(jnp.float32)
        + jnp.dot(attended, w_out, preferred_element_type=jnp.float32)
        + b_out
    ).astype(jnp.bfloat16)
    normed = layer_norm(hidden.astype(jnp.float32), final_gain, final_shift).astype(jnp.bfloat16)
    owners = mask_tokens.shape[0]
    capacity = mask_tokens.shape[1]
    per_source = capacity // owners
    spaces = lax.axis_size("space")
    spatial = patch_count * spaces
    own_index = lax.axis_index("tm") * spaces + lax.axis_index("space")
    owner_lists = jnp.take(mask_tokens, assignment, axis=0)
    listed = owner_lists >= 0
    clipped = jnp.maximum(owner_lists, 0)
    token_frame = clipped // spatial
    token_patch = clipped % spatial
    home_device = token_frame // frame_count * spaces + token_patch // patch_count
    local_row = token_frame % frame_count * patch_count + token_patch % patch_count
    mine = listed & (home_device == own_index)
    slot_index = jnp.cumsum(mine.astype(jnp.int32), axis=1) - 1
    wanted = mine[:, None, :] & (
        slot_index[:, None, :] == jnp.arange(per_source, dtype=jnp.int32)[None, :, None]
    )
    picks = jnp.sum(jnp.where(wanted, local_row[:, None, :], 0), axis=-1)
    present = jnp.any(wanted, axis=-1)
    own_home = lax.dynamic_index_in_dim(home_device, own_index, 0, keepdims=False)
    own_listed = lax.dynamic_index_in_dim(listed, own_index, 0, keepdims=False)
    entry_order = jnp.arange(capacity, dtype=jnp.int32)
    earlier = (
        (entry_order[:, None] < entry_order[None, :])
        & own_listed[:, None]
        & (own_home[:, None] == own_home[None, :])
    )
    entry_rank = jnp.sum(earlier.astype(jnp.int32), axis=0)
    where_from = jnp.where(own_listed, own_home * per_source + entry_rank, 0)
    outgoing = jnp.where(
        present[:, :, None], jnp.take(normed, picks, axis=0), jnp.zeros((), jnp.bfloat16)
    )
    arrived = lax.all_to_all(outgoing, ("tm", "space"), split_axis=0, concat_axis=0, tiled=True)
    row_table = arrived.reshape(owners * per_source, model_width)
    placed = jnp.take(row_table, where_from, axis=0)
    return jnp.where(own_listed[:, None], placed, jnp.zeros((), jnp.bfloat16))[None]


LANES = 128
WINDOW = 256
VMEM_LIMIT = 60 * 1024 * 1024
MESH = pl.DeviceIdType.MESH


def norm_rows(values, gain, shift):
    return layer_norm(values.astype(jnp.float32), gain, shift).astype(jnp.bfloat16)


def count_floor(values, size):
    return jnp.floor((values + 0.5) * (1.0 / size))


def small_dot(left, right):
    return jnp.dot(
        left.astype(jnp.bfloat16), right.astype(jnp.bfloat16), preferred_element_type=jnp.float32
    )


def fused_kernel(
    times,
    spaces,
    frames,
    patches,
    head_width,
    x_ref,
    gain_flat,
    shift_flat,
    w_qkv_ref,
    b_qkv_flat,
    w_out_ref,
    b_out_flat,
    final_gain_flat,
    final_shift_flat,
    lists_ref,
    assignment_ref,
    out_ref,
    own,
    x_all,
    k_all,
    v_all,
    w_q,
    w_k,
    w_v,
    w_out,
    normed,
    rows_f32,
    queries,
    sums,
    high,
    total,
    attended,
    attended_in,
    made_rows,
    back_rows,
    unpermute,
    b_qkv_ref,
    vectors,
    load_sem,
    own_sem,
    part_sem,
    side_sem,
    line_sem,
    recv,
    swap_sem,
    back_sem,
):
    me = lax.axis_index("tm")
    side = lax.axis_index("space")
    clip = lax.axis_index("clip")
    core = lax.rem(clip, 2)
    other = 1 - side
    partner = clip + 1 - 2 * core
    mate = me + 1 - 2 * lax.rem(me, 2)
    pair = lax.div(me, 2)
    far = lax.rem(me + 2, times)
    across = times - 1 - me
    active_core = lax.rem(me, 2)
    active = core == active_core
    idle = core != active_core
    inner = (me > 0) & (me < times - 1)
    left = me < times // 2
    rows, width = x_ref.shape
    quarter = rows // 4
    share = quarter // spaces
    owners, capacity = lists_ref.shape
    half_width = width // 2
    first_lane = half_width // LANES * LANES
    span = width - first_lane
    lane_skip = half_width - first_lane

    def core_clip(parity):
        return clip - core + parity

    column = pl.multiple_of(core * first_lane, LANES)
    loads = [
        pltpu.make_async_copy(
            w_qkv_ref.at[:, pl.ds(pl.multiple_of(part * width + column, LANES), span)],
            place,
            load_sem.at[part],
        )
        for part, place in ((1, w_k), (2, w_v), (0, w_q))
    ]
    loads.append(pltpu.make_async_copy(w_out_ref, w_out, load_sem.at[3]))
    for load in loads:
        load.start()

    barrier = pltpu.get_barrier_semaphore()

    def greet(**place):
        pl.semaphore_signal(barrier, inc=1, device_id=place, device_id_type=MESH)

    greet(clip=partner)
    for parity in range(2):
        greet(space=other, clip=core_clip(parity))
        greet(tm=mate, clip=core_clip(parity))
        greet(tm=far, clip=core_clip(parity))

        @pl.when(inner)
        def _():
            greet(tm=across, clip=core_clip(parity))

    b_qkv_ref[...] = b_qkv_flat[...].reshape(1, 3 * width)
    flats = (gain_flat, shift_flat, b_out_flat, final_gain_flat, final_shift_flat)
    for place, flat in enumerate(flats):
        vectors[place : place + 1, :] = flat[...].reshape(1, width)
    gain_ref, shift_ref, b_out_ref, final_gain_ref, final_shift_ref = (
        vectors.at[place : place + 1, :] for place in range(len(flats))
    )

    lists = lists_ref[...].astype(jnp.float32)
    list_places = lax.broadcasted_iota(jnp.int32, lists.shape, 0)

    def list_of(device):
        owner = assignment_ref[device]
        return jnp.sum(jnp.where(list_places == owner, lists, 0.0), axis=0, keepdims=True)

    spatial = patches * spaces
    base_token = (me * (frames * spatial) + side * patches).astype(jnp.float32)
    row = lax.broadcasted_iota(jnp.int32, (rows, 1), 0).astype(jnp.float32)
    row_frame = count_floor(row, patches)
    token = base_token + row_frame * spatial + (row - row_frame * patches)
    lane = lax.broadcasted_iota(jnp.int32, (rows, LANES), 1)
    member = jnp.zeros((rows, LANES), jnp.float32)
    taken = jnp.zeros((rows, 1), jnp.float32)
    for group in range(owners):
        parity, rest = divmod(group, owners // 2)
        group_pair, group_side = divmod(rest, spaces)
        device = (group_pair * 2 + parity) * spaces + group_side
        hit = jnp.max(
            jnp.where(token == list_of(device), 1.0, 0.0), axis=1, keepdims=True
        )
        member += jnp.where(lane == group, hit, 0.0)
        taken += hit
    member += jnp.where(lane == owners, 1.0 - taken, 0.0)
    square_row = lax.broadcasted_iota(jnp.int32, (rows, rows), 0)
    square_lane = lax.broadcasted_iota(jnp.int32, (rows, rows), 1)
    before = small_dot(jnp.where(square_lane < square_row, 1.0, 0.0), member)
    group_base = jnp.where(lane < owners, lane * share, 0).astype(jnp.float32)
    place_of = jnp.sum(member * (before + group_base), axis=1, keepdims=True)
    counts = jnp.sum(member, axis=0, keepdims=True)
    group_row = lax.broadcasted_iota(jnp.int32, (LANES, rows), 0)
    group_lane = lax.broadcasted_iota(jnp.int32, (LANES, rows), 1)
    in_group = (group_lane >= group_row * share) & (group_lane < (group_row + 1) * share)
    held = small_dot(jnp.broadcast_to(counts, (8, LANES)), jnp.where(in_group, 1.0, 0.0))
    slot = lax.broadcasted_iota(jnp.int32, (8, rows), 1).astype(jnp.float32)
    free = jnp.where(slot - count_floor(slot, share) * share >= held, 1.0, 0.0)
    free_before = small_dot(free, jnp.where(square_row < square_lane, 1.0, 0.0))
    free_place = jnp.where(free > 0.5, free_before, -1.0)
    chosen = jnp.where(taken > 0.5, slot[0:1], free_place[0:1]) == place_of
    permuted = lax.dot_general(
        jnp.where(chosen, 1.0, 0.0).astype(jnp.bfloat16),
        x_ref[...],
        (((0,), (0,)), ((), ())),
        preferred_element_type=jnp.float32,
    ).astype(jnp.bfloat16)
    for half in range(2):
        for part in range(2):
            start = (half * 2 + part) * quarter
            own[part, half] = permuted[start : start + quarter]

    @pl.when(active)
    def _():
        for half in range(2):
            for part in range(2):
                start = (half * 2 + part) * quarter
                x_all[me, part, side, half] = permuted[start : start + quarter]

    pl.semaphore_wait(barrier, 7 + 2 * inner.astype(jnp.int32))

    def remote(source, target, send, receive, place):
        return pltpu.make_async_remote_copy(
            source, target, send, receive, device_id=place, device_id_type=MESH
        )

    def own_copy(kind, part, half):
        place = {
            0: {"clip": partner},
            1: {"space": other, "clip": core_clip(half)},
            2: {"tm": jnp.where(active, far, mate), "clip": core_clip(half)},
            3: {"tm": across, "clip": core_clip(half)},
        }[kind]
        return remote(
            own.at[part, half],
            x_all.at[me, part, side, half],
            own_sem.at[kind, part, half],
            recv.at[me, part, side, half],
            place,
        )

    near_part = (pair, 1 - pair)
    line_part = (jnp.where(active, 1 - pair, pair), jnp.where(active, pair, 1 - pair))
    across_part = (1 - pair, pair)
    send_across = idle & inner

    def line_sends(phase):
        for half in range(2):
            own_copy(2, line_part[phase], half).start()

        @pl.when(send_across)
        def _():
            for half in range(2):
                own_copy(3, across_part[phase], half).start()

    def near_sends(phase):
        @pl.when(active)
        def _():
            for half in range(2):
                own_copy(1, near_part[phase], half).start()
            for half in range(2):
                own_copy(0, near_part[phase], half).start()

    line_sends(0)

    @pl.when(idle & jnp.logical_not(inner))
    def _():
        for half in range(2):
            own_copy(2, line_part[1], half).start()

    near_sends(0)

    order = (
        me,
        mate,
        jnp.where(left, times // 2, times // 2 - 1),
        jnp.where(left, times - 1, 0),
    )

    def part_copy(place, phase, from_side, across_side):
        spot = (order[place], near_part[phase], from_side, core)
        return remote(
            x_all.at[spot], x_all.at[spot], part_sem.at[place, phase, across_side],
            recv.at[spot], {"clip": partner},
        )

    def side_copy(place, phase):
        spot = (order[place], near_part[phase], side, core)
        return remote(
            x_all.at[spot], x_all.at[spot], side_sem.at[place, phase],
            recv.at[spot], {"space": other},
        )

    def line_copy(phase):
        spot = (mate, near_part[phase], side, core)
        return remote(
            x_all.at[spot], x_all.at[spot], line_sem.at[phase], recv.at[spot], {"tm": far}
        )

    def landed(place, phase, from_side, half):
        spot = (order[place], near_part[phase], from_side, half)
        remote(
            x_all.at[spot], x_all.at[spot], part_sem.at[place, phase, 0],
            recv.at[spot], {"clip": partner},
        ).wait_recv()

    def arrive(place, phase):
        if place == 1 and phase == 1:

            @pl.when(jnp.logical_not(inner))
            def _():
                landed(place, phase, side, core)

        else:
            landed(place, phase, side, core)
        side_copy(place, phase).start()
        part_copy(place, phase, side, 0).start()
        if place == 1:
            if phase == 0:

                @pl.when(inner)
                def _():
                    landed(1, 1, side, core)
                    line_copy(1).start()

            else:

                @pl.when(inner)
                def _():
                    line_copy(0).start()

    def gather(place, phase):
        landed(place, phase, other, core)
        part_copy(place, phase, other, 1).start()
        if place == 0:

            @pl.when(idle)
            def _():
                landed(place, phase, side, 0)
                landed(place, phase, side, 1)

        else:
            landed(place, phase, side, 1 - core)
        landed(place, phase, other, 1 - core)

    def project(place, phase):
        gather(place, phase)
        normed[:rows, :] = norm_rows(
            x_all[order[place], near_part[phase]].reshape(rows, width),
            gain_ref[...],
            shift_ref[...],
        )
        start = (phase * times + place) * rows
        for part, weight, target in ((1, w_k, k_all), (2, w_v, v_all)):
            bias = b_qkv_ref[:, pl.ds(pl.multiple_of(part * width + column, LANES), span)]
            target[start : start + rows, :] = (
                jnp.dot(normed[:rows, :], weight[...], preferred_element_type=jnp.float32) + bias
            ).astype(jnp.bfloat16)

    score_scale = math.log2(math.e) / math.sqrt(head_width)
    half_heads = HEADS // 2
    groups = []
    head = 0
    while head < half_heads:
        base = min(head * head_width // LANES, span // LANES - 2) * LANES
        count = 1
        while (
            head + count < half_heads
            and (head + count + 1) * head_width + lane_skip <= base + WINDOW
        ):
            count += 1
        groups.append((base, range(head, head + count)))
        head += count
    skip = core * lane_skip

    def head_masks(height, base, heads):
        place = lax.broadcasted_iota(jnp.int32, (height, WINDOW), 1) + (base - skip)
        return [(place >= h * head_width) & (place < (h + 1) * head_width) for h in heads]

    def scores_of(row_slice, base, masks, key_start, key_end):
        window = queries[row_slice, base : base + WINDOW].astype(jnp.float32)
        stacked = jnp.concatenate(
            [jnp.where(mask, window, 0.0).astype(jnp.bfloat16) for mask in masks]
        )
        return lax.dot_general(
            stacked,
            k_all[key_start:key_end, base : base + WINDOW],
            (((1,), (1,)), ((), ())),
            preferred_element_type=jnp.float32,
        )

    split = times * rows
    all_keys = 2 * split

    def attend_first():
        sums[...] = jnp.zeros_like(sums)
        height = 2 * rows
        for base, heads in groups:
            masks = head_masks(height, base, heads)
            scores = scores_of(pl.ds(0, height), base, masks, 0, split)
            top = jnp.max(scores, axis=1, keepdims=True)
            weights = jnp.exp2((scores - top) * score_scale)
            summed = jnp.dot(
                weights.astype(jnp.bfloat16),
                v_all[0:split, base : base + WINDOW],
                preferred_element_type=jnp.float32,
            )
            counted = jnp.sum(weights, axis=1, keepdims=True)
            for place, h in enumerate(heads):
                part = slice(place * height, (place + 1) * height)
                high[h] = top[part]
                total[h] = counted[part]
                sums[:, base : base + WINDOW] += jnp.where(masks[place], summed[part], 0.0)

    def attend_rest(start):
        row_slice = pl.ds(start, rows)
        attended[row_slice, :] = jnp.zeros((rows, span), jnp.bfloat16)
        for base, heads in groups:
            masks = head_masks(rows, base, heads)
            scores = scores_of(row_slice, base, masks, split, all_keys)
            old = jnp.concatenate([high[h, row_slice, :] for h in heads])
            top = jnp.maximum(old, jnp.max(scores, axis=1, keepdims=True))
            weights = jnp.exp2((scores - top) * score_scale)
            factor = jnp.exp2((old - top) * score_scale)
            counted = jnp.concatenate([total[h, row_slice, :] for h in heads])
            counted = counted * factor + jnp.sum(weights, axis=1, keepdims=True)
            summed = jnp.dot(
                weights.astype(jnp.bfloat16),
                v_all[split:all_keys, base : base + WINDOW],
                preferred_element_type=jnp.float32,
            )
            carried = sums[row_slice, base : base + WINDOW]
            for place, h in enumerate(heads):
                part = slice(place * rows, (place + 1) * rows)
                result = (carried * factor[part] + summed[part]) / counted[part]
                kept = attended[row_slice, base : base + WINDOW].astype(jnp.float32)
                attended[row_slice, base : base + WINDOW] = jnp.where(
                    masks[place], result, kept
                ).astype(jnp.bfloat16)

    def make_queries():
        for parity in range(2):
            for block in range(times):
                for from_side in range(spaces):
                    piece = x_all[block, pair, from_side, parity].astype(jnp.float32)
                    start = parity * rows + (block * spaces + from_side) * share
                    rows_f32[start : start + share, :] = jnp.where(
                        side == 0, piece[:share], piece[share:]
                    )
        normed[...] = norm_rows(rows_f32[...], gain_ref[...], shift_ref[...])
        queries[...] = (
            jnp.dot(normed[...], w_q[...], preferred_element_type=jnp.float32)
            + b_qkv_ref[:, pl.ds(column, span)]
        ).astype(jnp.bfloat16)

    arrive(1, 0)
    line_sends_late = active | inner

    @pl.when(line_sends_late)
    def _():
        for half in range(2):
            own_copy(2, line_part[1], half).start()

    @pl.when(send_across)
    def _():
        for half in range(2):
            own_copy(3, across_part[1], half).start()

    near_sends(1)

    token_row = list_of(me * spaces + side)
    diagonal = square_row == square_lane

    def upright(values):
        return jnp.sum(jnp.where(diagonal, values, 0.0), axis=1, keepdims=True)

    def home_of(tokens):
        frame = count_floor(tokens, spatial)
        patch = tokens - frame * spatial
        block = count_floor(frame, frames)
        from_side = count_floor(patch, patches)
        inside = (frame - block * frames) * patches + patch - from_side * patches
        return block * spaces + from_side, inside

    token_column = upright(token_row)
    home_row, inside_row = home_of(token_row)
    home_column, inside_column = home_of(token_column)
    earlier = (
        (home_row == home_column) & (inside_row < inside_column) & (token_row >= 0)
    )
    rank = jnp.sum(jnp.where(earlier, 1.0, 0.0), axis=1, keepdims=True)
    wanted = home_column * share + rank
    found = (square_lane.astype(jnp.float32) == wanted) & (token_column >= 0)
    unpermute[...] = jnp.where(found, 1.0, 0.0).astype(jnp.bfloat16)

    for load in loads[:2]:
        load.wait()
    project(0, 0)
    arrive(2, 0)
    project(1, 0)
    arrive(3, 0)
    project(2, 0)
    arrive(1, 1)
    project(3, 0)
    loads[2].wait()
    make_queries()
    arrive(2, 1)
    project(0, 1)
    attend_first()
    arrive(3, 1)
    project(1, 1)
    project(2, 1)
    project(3, 1)
    loads[3].wait()

    def swap_copy(start):
        return remote(
            attended.at[pl.ds(start, rows)], attended_in, swap_sem.at[0], swap_sem.at[1],
            {"clip": partner},
        )

    back = remote(
        made_rows, back_rows, back_sem.at[0], back_sem.at[1],
        {"tm": mate, "clip": core_clip(1 - core)},
    )

    def finish(step, carried):
        owner = jnp.where(step == 0, 1 - active_core, active_core)
        start = pl.multiple_of(owner * rows, rows)
        attend_rest(start)

        @pl.when(owner != core)
        def _():
            swap_copy(start).start()

        @pl.when(owner == core)
        def _():
            swap_copy(start).wait_recv()
            mine = jnp.dot(
                attended[pl.ds(start, rows), :],
                w_out[pl.ds(pl.multiple_of(core * first_lane, LANES), span), :],
                preferred_element_type=jnp.float32,
            )
            theirs = jnp.dot(
                attended_in[...],
                w_out[pl.ds(pl.multiple_of((1 - core) * first_lane, LANES), span), :],
                preferred_element_type=jnp.float32,
            )
            hidden = (
                rows_f32[pl.ds(start, rows), :] + mine + theirs + b_out_ref[...]
            ).astype(jnp.bfloat16)
            made_rows[...] = layer_norm(
                hidden.astype(jnp.float32), final_gain_ref[...], final_shift_ref[...]
            ).astype(jnp.bfloat16)

            @pl.when(idle)
            def _():
                back.start()

        return carried

    lax.fori_loop(0, 2, finish, 0)

    def give(source):
        out_ref[0] = jnp.dot(
            unpermute[...], source[...], preferred_element_type=jnp.float32
        ).astype(jnp.bfloat16)

    @pl.when(active)
    def _():
        give(made_rows)

    @pl.when(idle)
    def _():
        back.wait_recv()
        give(back_rows)
        back.wait_send()

    swap_copy(pl.multiple_of((1 - core) * rows, rows)).wait_send()
    for phase in range(2):
        for half in range(2):
            own_copy(2, line_part[phase], half).wait_send()

            @pl.when(send_across)
            def _():
                own_copy(3, across_part[phase], half).wait_send()

            @pl.when(active)
            def _():
                own_copy(1, near_part[phase], half).wait_send()
                own_copy(0, near_part[phase], half).wait_send()

        for place in range(times):
            part_copy(place, phase, other, 1).wait_send()
            if place:
                part_copy(place, phase, side, 0).wait_send()
                side_copy(place, phase).wait_send()

        @pl.when(inner)
        def _():
            line_copy(phase).wait_send()


def fits_fused(times, spaces, clips, rows, width, owners, capacity):
    all_rows = times * spaces * rows
    held = 2 * (all_rows * width * 3 + width * width * 4 + 6 * rows * width)
    held += 4 * capacity * (width * 6 + all_rows * 6)
    share = capacity // owners
    return (
        spaces == 2
        and times == 4
        and clips % 2 == 0
        and held < VMEM_LIMIT
        and width % LANES == 0
        and HEADS % 2 == 0
        and width // HEADS <= LANES
        and owners == times * spaces
        and share * owners == capacity == rows
        and share % 8 == 0
        and rows % 64 == 0
    )


def fused_local(
    activations,
    attn_gain,
    attn_shift,
    w_qkv,
    b_qkv,
    w_out,
    b_out,
    final_gain,
    final_shift,
    mask_tokens,
    assignment,
):
    frames, patches, width = activations.shape
    rows = frames * patches
    times = lax.axis_size("tm")
    spaces = lax.axis_size("space")
    clips = lax.axis_size("clip")
    owners, capacity = mask_tokens.shape
    if not fits_fused(times, spaces, clips, rows, width, owners, capacity):
        return local(
            activations, attn_gain, attn_shift, w_qkv, b_qkv, w_out, b_out,
            final_gain, final_shift, mask_tokens, assignment,
        )
    half_width = width // 2
    span = width - half_width // LANES * LANES
    quarter = rows // 4
    keys = times * spaces * rows
    half_heads = HEADS // 2
    vmem = pl.BlockSpec(memory_space=pltpu.VMEM)
    hbm = pl.BlockSpec(memory_space=pl.ANY)
    smem = pl.BlockSpec(memory_space=pltpu.SMEM)
    bf16, f32 = jnp.bfloat16, jnp.float32
    dma = pltpu.SemaphoreType.DMA
    return pl.pallas_call(
        functools.partial(fused_kernel, times, spaces, frames, patches, width // HEADS),
        out_shape=jax.ShapeDtypeStruct((1, capacity, width), bf16),
        in_specs=[vmem, vmem, vmem, hbm, vmem, hbm, vmem, vmem, vmem, vmem, smem],
        out_specs=vmem,
        scratch_shapes=[
            pltpu.VMEM((2, 2, quarter, width), bf16),
            pltpu.VMEM((times, 2, spaces, 2, quarter, width), bf16),
            pltpu.VMEM((keys, span), bf16),
            pltpu.VMEM((keys, span), bf16),
            pltpu.VMEM((width, span), bf16),
            pltpu.VMEM((width, span), bf16),
            pltpu.VMEM((width, span), bf16),
            pltpu.VMEM((width, width), bf16),
            pltpu.VMEM((2 * rows, width), bf16),
            pltpu.VMEM((2 * rows, width), f32),
            pltpu.VMEM((2 * rows, span), bf16),
            pltpu.VMEM((2 * rows, span), f32),
            pltpu.VMEM((half_heads, 2 * rows, 1), f32),
            pltpu.VMEM((half_heads, 2 * rows, 1), f32),
            pltpu.VMEM((2 * rows, span), bf16),
            pltpu.VMEM((rows, span), bf16),
            pltpu.VMEM((rows, width), bf16),
            pltpu.VMEM((rows, width), bf16),
            pltpu.VMEM((rows, rows), bf16),
            pltpu.VMEM((1, 3 * width), f32),
            pltpu.VMEM((5, width), f32),
            dma((4,)),
            dma((4, 2, 2)),
            dma((times, 2, 2)),
            dma((times, 2)),
            dma((2,)),
            dma((times, 2, spaces, 2)),
            dma((2,)),
            dma((2,)),
        ],
        compiler_params=pltpu.CompilerParams(
            collective_id=0, has_side_effects=True, vmem_limit_bytes=VMEM_LIMIT
        ),
    )(
        activations.reshape(rows, width),
        attn_gain,
        attn_shift,
        w_qkv,
        b_qkv,
        w_out,
        b_out,
        final_gain,
        final_shift,
        mask_tokens,
        assignment,
    )


def solution(mesh):
    in_specs = (
        P(("clip", "tm"), "space", None),
        P(),
        P(),
        P(),
        P(),
        P(),
        P(),
        P(),
        P(),
        P("clip", None),
        P("clip"),
    )
    out_specs = P(("clip", "tm", "space"), None, None)
    return jax.shard_map(fused_local, mesh=mesh, in_specs=in_specs, out_specs=out_specs, check_vma=False)
```

time: 65.6 us -> 65.8 us (level)
  the two profiles are of different devices: /device:TPU:0 before, /device:TPU:1 now
where the time goes in v2:
time: 65.8 us; the launch traced here: 65.6 us
  Pallas kernels  63.7 us (97%)
  local copies, waits for them, and re-layouts  1.89 us (3%)
    pallas_call x1, Pallas kernels, fused_local(): pl.pallas_call(functools.partial(fused_kernel, times, spaces, frames, pat...  63.7 us
    unnamed x1, local copies, waits for them, and re-layouts  1.89 us

profile of v2, /device:TPU:1, one launch (start us, length us, event | category | flops | bytes accessed | tf_op | source)
XLA Modules:
  0.0 65.6 jit_solution(11468197404557786159)
XLA Ops:
  0.0 63.7 %shard_map.109 = bf16[1,192,1408]{2,1,0:T(8,128)(2,1)} custom-call(bf16[192,1408]{1,0:T(8,128)(2,1)} %bitcast.1, f32[1408]{0:T(1024)} %gain_flat.1, f32[1408]{0:T(1024)} %shift_flat.1, bf16[1408,4224]{1,0:T(8,128)(2,1)} %w_qkv_ref.1, f32[4224]{0:T(1024)} %b_qkv_flat.1, bf16[1408,1408]{1,0:T(8,128)(2,1)} %w_out_ref.1, f32[1408]{0:T(1024)} %b_out_flat.1, ...), custom_call_target="tpu_custom_call" | custom-call | tf_op jit(solution)/shard_map/pallas_call | solution.py:794
  63.7 1.9 %copy.13 = bf16[1,192,1408]{2,1,0:T(8,128)(2,1)} copy(bf16[1,192,1408]{2,1,0:T(8,128)(2,1)} %shard_map.109) | data formatting | bytes 1081344

commit v3 on v2

--- a/solution.py
+++ b/solution.py
@@ -214,8 +214,6 @@
     rows_f32,
     queries,
     sums,
-    high,
-    total,
     attended,
     attended_in,
     made_rows,
@@ -376,8 +374,7 @@
         )
 
     near_part = (pair, 1 - pair)
-    line_part = (jnp.where(active, 1 - pair, pair), jnp.where(active, pair, 1 - pair))
-    across_part = (1 - pair, pair)
+    line_part = (1 - pair, pair)
     send_across = idle & inner
 
     def line_sends(phase):
@@ -387,7 +384,7 @@
         @pl.when(send_across)
         def _():
             for half in range(2):
-                own_copy(3, across_part[phase], half).start()
+                own_copy(3, line_part[phase], half).start()
 
     def near_sends(phase):
         @pl.when(active)
@@ -398,13 +395,9 @@
                 own_copy(0, near_part[phase], half).start()
 
     line_sends(0)
-
-    @pl.when(idle & jnp.logical_not(inner))
-    def _():
-        for half in range(2):
-            own_copy(2, line_part[1], half).start()
-
     near_sends(0)
+    line_sends(1)
+    near_sends(1)
 
     order = (
         me,
@@ -441,33 +434,21 @@
         ).wait_recv()
 
     def arrive(place, phase):
-        if place == 1 and phase == 1:
-
-            @pl.when(jnp.logical_not(inner))
+        landed(place, phase, side, core)
+        if place == 1:
+
+            @pl.when(inner)
             def _():
-                landed(place, phase, side, core)
-
-        else:
-            landed(place, phase, side, core)
+                line_copy(phase).start()
+
         side_copy(place, phase).start()
         part_copy(place, phase, side, 0).start()
-        if place == 1:
-            if phase == 0:
-
-                @pl.when(inner)
-                def _():
-                    landed(1, 1, side, core)
-                    line_copy(1).start()
-
-            else:
-
-                @pl.when(inner)
-                def _():
-                    line_copy(0).start()
-
-    def gather(place, phase):
+
+    def relay(place, phase):
         landed(place, phase, other, core)
         part_copy(place, phase, other, 1).start()
+
+    def gather(place, phase):
         if place == 0:
 
             @pl.when(idle)
@@ -480,7 +461,8 @@
         landed(place, phase, other, 1 - core)
 
     def project(place, phase):
-        gather(place, phase)
+        if (place, phase) != (3, 0):
+            gather(place, phase)
         normed[:rows, :] = norm_rows(
             x_all[order[place], near_part[phase]].reshape(rows, width),
             gain_ref[...],
@@ -525,54 +507,29 @@
             preferred_element_type=jnp.float32,
         )
 
-    split = times * rows
-    all_keys = 2 * split
-
-    def attend_first():
-        sums[...] = jnp.zeros_like(sums)
-        height = 2 * rows
+    all_keys = 2 * times * rows
+
+    def attend_all(start, height):
+        row_slice = pl.ds(start, height)
+        sums[row_slice, :] = jnp.zeros((height, span), jnp.float32)
         for base, heads in groups:
             masks = head_masks(height, base, heads)
-            scores = scores_of(pl.ds(0, height), base, masks, 0, split)
+            scores = scores_of(row_slice, base, masks, 0, all_keys)
             top = jnp.max(scores, axis=1, keepdims=True)
             weights = jnp.exp2((scores - top) * score_scale)
+            counted = jnp.sum(weights, axis=1, keepdims=True)
             summed = jnp.dot(
                 weights.astype(jnp.bfloat16),
-                v_all[0:split, base : base + WINDOW],
+                v_all[:, base : base + WINDOW],
                 preferred_element_type=jnp.float32,
-            )
-            counted = jnp.sum(weights, axis=1, keepdims=True)
-            for place, h in enumerate(heads):
-                part = slice(place * height, (place + 1) * height)
-                high[h] = top[part]
-                total[h] = counted[part]
-                sums[:, base : base + WINDOW] += jnp.where(masks[place], summed[part], 0.0)
-
-    def attend_rest(start):
-        row_slice = pl.ds(start, rows)
-        attended[row_slice, :] = jnp.zeros((rows, span), jnp.bfloat16)
-        for base, heads in groups:
-            masks = head_masks(rows, base, heads)
-            scores = scores_of(row_slice, base, masks, split, all_keys)
-            old = jnp.concatenate([high[h, row_slice, :] for h in heads])
-            top = jnp.maximum(old, jnp.max(scores, axis=1, keepdims=True))
-            weights = jnp.exp2((scores - top) * score_scale)
-            factor = jnp.exp2((old - top) * score_scale)
-            counted = jnp.concatenate([total[h, row_slice, :] for h in heads])
-            counted = counted * factor + jnp.sum(weights, axis=1, keepdims=True)
-            summed = jnp.dot(
-                weights.astype(jnp.bfloat16),
-                v_all[split:all_keys, base : base + WINDOW],
-                preferred_element_type=jnp.float32,
-            )
-            carried = sums[row_slice, base : base + WINDOW]
-            for place, h in enumerate(heads):
-                part = slice(place * rows, (place + 1) * rows)
-                result = (carried * factor[part] + summed[part]) / counted[part]
-                kept = attended[row_slice, base : base + WINDOW].astype(jnp.float32)
-                attended[row_slice, base : base + WINDOW] = jnp.where(
-                    masks[place], result, kept
-                ).astype(jnp.bfloat16)
+            ) / counted
+            result = jnp.where(masks[0], summed[:height], 0.0)
+            for place in range(1, len(heads)):
+                result = jnp.where(
+                    masks[place], summed[place * height : (place + 1) * height], result
+                )
+            sums[row_slice, base : base + WINDOW] += result
+        attended[row_slice, :] = sums[row_slice, :].astype(jnp.bfloat16)
 
     def make_queries():
         for parity in range(2):
@@ -589,20 +546,8 @@
             + b_qkv_ref[:, pl.ds(column, span)]
         ).astype(jnp.bfloat16)
 
+    arrive(1, 1)
     arrive(1, 0)
-    line_sends_late = active | inner
-
-    @pl.when(line_sends_late)
-    def _():
-        for half in range(2):
-            own_copy(2, line_part[1], half).start()
-
-    @pl.when(send_across)
-    def _():
-        for half in range(2):
-            own_copy(3, across_part[1], half).start()
-
-    near_sends(1)
 
     token_row = list_of(me * spaces + side)
     diagonal = square_row == square_lane
@@ -631,21 +576,28 @@
 
     for load in loads[:2]:
         load.wait()
+    relay(0, 0)
     project(0, 0)
+    relay(0, 1)
+    project(0, 1)
+    relay(1, 1)
     arrive(2, 0)
+    project(1, 1)
+    relay(1, 0)
     project(1, 0)
+    arrive(2, 1)
+    relay(2, 0)
+    project(2, 0)
     arrive(3, 0)
-    project(2, 0)
-    arrive(1, 1)
+    relay(2, 1)
+    project(2, 1)
+    relay(3, 0)
+    arrive(3, 1)
+    loads[2].wait()
+    gather(3, 0)
+    make_queries()
+    relay(3, 1)
     project(3, 0)
-    loads[2].wait()
-    make_queries()
-    arrive(2, 1)
-    project(0, 1)
-    attend_first()
-    arrive(3, 1)
-    project(1, 1)
-    project(2, 1)
     project(3, 1)
     loads[3].wait()
 
@@ -655,15 +607,19 @@
             {"clip": partner},
         )
 
-    back = remote(
-        made_rows, back_rows, back_sem.at[0], back_sem.at[1],
-        {"tm": mate, "clip": core_clip(1 - core)},
-    )
+    chunk = rows // 2
+
+    def back_copy(step):
+        piece = pl.ds(pl.multiple_of(step * chunk, chunk), chunk)
+        return remote(
+            made_rows.at[piece], back_rows.at[piece], back_sem.at[0, step], back_sem.at[1, step],
+            {"tm": mate, "clip": core_clip(1 - core)},
+        )
 
     def finish(step, carried):
         owner = jnp.where(step == 0, 1 - active_core, active_core)
         start = pl.multiple_of(owner * rows, rows)
-        attend_rest(start)
+        attend_all(start, rows)
 
         @pl.when(owner != core)
         def _():
@@ -671,27 +627,38 @@
 
         @pl.when(owner == core)
         def _():
-            swap_copy(start).wait_recv()
-            mine = jnp.dot(
-                attended[pl.ds(start, rows), :],
-                w_out[pl.ds(pl.multiple_of(core * first_lane, LANES), span), :],
-                preferred_element_type=jnp.float32,
-            )
-            theirs = jnp.dot(
-                attended_in[...],
-                w_out[pl.ds(pl.multiple_of((1 - core) * first_lane, LANES), span), :],
-                preferred_element_type=jnp.float32,
-            )
-            hidden = (
-                rows_f32[pl.ds(start, rows), :] + mine + theirs + b_out_ref[...]
-            ).astype(jnp.bfloat16)
-            made_rows[...] = layer_norm(
-                hidden.astype(jnp.float32), final_gain_ref[...], final_shift_ref[...]
-            ).astype(jnp.bfloat16)
-
-            @pl.when(idle)
-            def _():
-                back.start()
+            def close(step, carried):
+                inside = pl.multiple_of(step * chunk, chunk)
+                piece = pl.ds(pl.multiple_of(start + inside, chunk), chunk)
+                mine = jnp.dot(
+                    attended[piece, :],
+                    w_out[pl.ds(pl.multiple_of(core * first_lane, LANES), span), :],
+                    preferred_element_type=jnp.float32,
+                )
+
+                @pl.when(step == 0)
+                def _():
+                    swap_copy(start).wait_recv()
+
+                theirs = jnp.dot(
+                    attended_in[pl.ds(inside, chunk), :],
+                    w_out[pl.ds(pl.multiple_of((1 - core) * first_lane, LANES), span), :],
+                    preferred_element_type=jnp.float32,
+                )
+                hidden = (
+                    rows_f32[piece, :] + mine + theirs + b_out_ref[...]
+                ).astype(jnp.bfloat16)
+                made_rows[pl.ds(inside, chunk), :] = layer_norm(
+                    hidden.astype(jnp.float32), final_gain_ref[...], final_shift_ref[...]
+                ).astype(jnp.bfloat16)
+
+                @pl.when(idle)
+                def _():
+                    back_copy(step).start()
+
+                return carried
+
+            lax.fori_loop(0, 2, close, 0)
 
         return carried
 
@@ -708,9 +675,11 @@
 
     @pl.when(idle)
     def _():
-        back.wait_recv()
+        for step in range(2):
+            back_copy(step).wait_recv()
         give(back_rows)
-        back.wait_send()
+        for step in range(2):
+            back_copy(step).wait_send()
 
     swap_copy(pl.multiple_of((1 - core) * rows, rows)).wait_send()
     for phase in range(2):
@@ -719,7 +688,7 @@
 
             @pl.when(send_across)
             def _():
-                own_copy(3, across_part[phase], half).wait_send()
+                own_copy(3, line_part[phase], half).wait_send()
 
             @pl.when(active)
             def _():
@@ -785,7 +754,6 @@
     span = width - half_width // LANES * LANES
     quarter = rows // 4
     keys = times * spaces * rows
-    half_heads = HEADS // 2
     vmem = pl.BlockSpec(memory_space=pltpu.VMEM)
     hbm = pl.BlockSpec(memory_space=pl.ANY)
     smem = pl.BlockSpec(memory_space=pltpu.SMEM)
@@ -809,8 +777,6 @@
             pltpu.VMEM((2 * rows, width), f32),
             pltpu.VMEM((2 * rows, span), bf16),
             pltpu.VMEM((2 * rows, span), f32),
-            pltpu.VMEM((half_heads, 2 * rows, 1), f32),
-            pltpu.VMEM((half_heads, 2 * rows, 1), f32),
             pltpu.VMEM((2 * rows, span), bf16),
             pltpu.VMEM((rows, span), bf16),
             pltpu.VMEM((rows, width), bf16),
@@ -825,7 +791,7 @@
             dma((2,)),
             dma((times, 2, spaces, 2)),
             dma((2,)),
-            dma((2,)),
+            dma((2, 2)),
         ],
         compiler_params=pltpu.CompilerParams(
             collective_id=0, has_side_effects=True, vmem_limit_bytes=VMEM_LIMIT

time: 65.8 us -> 60.1 us (0.913)
  the two profiles are of different devices: /device:TPU:1 before, /device:TPU:0 now
where the time goes in v3:
time: 60.1 us; the launch traced here: 59.1 us
  Pallas kernels  57.2 us (95%)
  local copies, waits for them, and re-layouts  1.89 us (3%)
    pallas_call x1, Pallas kernels, fused_local(): pl.pallas_call(functools.partial(fused_kernel, times, spaces, frames, pat...  57.2 us
    unnamed x1, local copies, waits for them, and re-layouts  1.89 us

profile of v3, /device:TPU:0, one launch (start us, length us, event | category | flops | bytes accessed | tf_op | source)
XLA Modules:
  0.0 59.1 jit_solution(16174057504129732727)
XLA Ops:
  0.0 57.2 %shard_map.109 = bf16[1,192,1408]{2,1,0:T(8,128)(2,1)} custom-call(bf16[192,1408]{1,0:T(8,128)(2,1)} %bitcast.1, f32[1408]{0:T(1024)} %gain_flat.1, f32[1408]{0:T(1024)} %shift_flat.1, bf16[1408,4224]{1,0:T(8,128)(2,1)} %w_qkv_ref.1, f32[4224]{0:T(1024)} %b_qkv_flat.1, bf16[1408,1408]{1,0:T(8,128)(2,1)} %w_out_ref.1, f32[1408]{0:T(1024)} %b_out_flat.1, ...), custom_call_target="tpu_custom_call" | custom-call | tf_op jit(solution)/shard_map/pallas_call | solution.py:762
  57.2 1.9 %copy.13 = bf16[1,192,1408]{2,1,0:T(8,128)(2,1)} copy(bf16[1,192,1408]{2,1,0:T(8,128)(2,1)} %shard_map.109) | data formatting | bytes 1081344

commit v4 on v3

--- a/solution.py
+++ b/solution.py
@@ -267,8 +267,6 @@
         for part, place in ((1, w_k), (2, w_v), (0, w_q))
     ]
     loads.append(pltpu.make_async_copy(w_out_ref, w_out, load_sem.at[3]))
-    for load in loads:
-        load.start()
 
     barrier = pltpu.get_barrier_semaphore()
 
@@ -394,10 +392,12 @@
             for half in range(2):
                 own_copy(0, near_part[phase], half).start()
 
+    near_sends(0)
     line_sends(0)
-    near_sends(0)
+    near_sends(1)
     line_sends(1)
-    near_sends(1)
+    for load in loads:
+        load.start()
 
     order = (
         me,
@@ -517,12 +517,12 @@
             scores = scores_of(row_slice, base, masks, 0, all_keys)
             top = jnp.max(scores, axis=1, keepdims=True)
             weights = jnp.exp2((scores - top) * score_scale)
-            counted = jnp.sum(weights, axis=1, keepdims=True)
+            inverse = 1.0 / jnp.sum(weights, axis=1, keepdims=True)
             summed = jnp.dot(
                 weights.astype(jnp.bfloat16),
                 v_all[:, base : base + WINDOW],
                 preferred_element_type=jnp.float32,
-            ) / counted
+            ) * inverse
             result = jnp.where(masks[0], summed[:height], 0.0)
             for place in range(1, len(heads)):
                 result = jnp.where(

time: 60.1 us -> 60 us (level)
  no operation moved by 1% of the time
where the time goes in v4:
time: 60 us; the launch traced here: 59.1 us
  Pallas kernels  57.2 us (95%)
  local copies, waits for them, and re-layouts  1.89 us (3%)
    pallas_call x1, Pallas kernels, fused_local(): pl.pallas_call(functools.partial(fused_kernel, times, spaces, frames, pat...  57.2 us
    unnamed x1, local copies, waits for them, and re-layouts  1.89 us

profile of v4, /device:TPU:0, one launch (start us, length us, event | category | flops | bytes accessed | tf_op | source)
XLA Modules:
  0.0 59.1 jit_solution(16180107706867182630)
XLA Ops:
  0.0 57.2 %shard_map.109 = bf16[1,192,1408]{2,1,0:T(8,128)(2,1)} custom-call(bf16[192,1408]{1,0:T(8,128)(2,1)} %bitcast.1, f32[1408]{0:T(1024)} %gain_flat.1, f32[1408]{0:T(1024)} %shift_flat.1, bf16[1408,4224]{1,0:T(8,128)(2,1)} %w_qkv_ref.1, f32[4224]{0:T(1024)} %b_qkv_flat.1, bf16[1408,1408]{1,0:T(8,128)(2,1)} %w_out_ref.1, f32[1408]{0:T(1024)} %b_out_flat.1, ...), custom_call_target="tpu_custom_call" | custom-call | tf_op jit(solution)/shard_map/pallas_call | solution.py:762
  57.2 1.9 %copy.13 = bf16[1,192,1408]{2,1,0:T(8,128)(2,1)} copy(bf16[1,192,1408]{2,1,0:T(8,128)(2,1)} %shard_map.109) | data formatting | bytes 1081344
